TPU v7x, 128 devices: a whole 4x4x4 slice. The times are simulated.
128 devices in a mesh: shard: 64 (over z, y, x), tensor: 2 (over core).
Axes of the slice: x: 4, y: 4, z: 4, core: 2. Of those that a mesh axis runs over, the one named last changes fastest.
Arguments:
- weights: float32 [128, 512, 512], P(None, 'shard', 'tensor'), may hold values from -0.25 to 0.25
- gradient: float32 [128, 512, 512], P(None, 'shard', 'tensor'), may hold values from -40 to 40
- first_moment: float32 [128, 512, 512], P(None, 'shard', 'tensor'), may hold values from -6 to 6
- second_moment: float32 [128, 512, 512], P(None, 'shard', 'tensor'), may hold values from 0.25 to 4
- left_stat: float32 [128, 512, 512], P(None, 'shard', 'tensor'), may hold values from -4 to 16, as said below
- right_stat: float32 [128, 512, 512], P(None, 'shard', 'tensor'), may hold values from -4 to 16, as said below
- left_basis: float32 [128, 512, 512], P(None, 'shard', 'tensor'), may hold values from -0.7 to 1.7
- right_basis: float32 [128, 512, 512], P(None, 'shard', 'tensor'), may hold values from -0.7 to 1.7
Outputs:
- new_weights: float32 [128, 512, 512], P(None, 'shard', 'tensor')
- new_first: float32 [128, 512, 512], P(None, 'shard', 'tensor')
- new_second: float32 [128, 512, 512], P(None, 'shard', 'tensor')
- new_left_stat: float32 [128, 512, 512], P(None, 'shard', 'tensor')
- new_right_stat: float32 [128, 512, 512], P(None, 'shard', 'tensor')
- new_left_basis: float32 [128, 512, 512], P(None, 'shard', 'tensor')
- new_right_basis: float32 [128, 512, 512], P(None, 'shard', 'tensor')
Inputs may be any that keep to these rules, and one draw needn't show every extreme that they name: `left_stat`: symmetric. `right_stat`: symmetric.
All inputs are finite; a program needn't handle non-finite values.
Results may differ from a plain program's by a relative error of at most 0.0003.
Values sent between devices are 32-bit elements; how exact they have to be, the bound alone decides.
A program may use at most 128 MiB of HBM per device.

v0:
```python
import jax
import jax.numpy as jnp
from jax import lax
from jax.sharding import PartitionSpec as P

NS_STEPS = 5


BETA_ONE = 0.9
BETA_TWO = 0.99
BETA_STAT = 0.95
ADAM_EPS = 1e-08
STEP_RATE = 0.01
NORM_EPS = 1e-06
COEF_A = 3.4445
COEF_B = -4.775
COEF_C = 2.0315
HIGH = lax.Precision.HIGHEST


def contract(form, left, right):
    return jnp.einsum(form, left, right, precision=HIGH, preferred_element_type=jnp.float32)


def newton_step(iterate, iterate_full):
    square = contract("mki,mkj->mij", iterate_full, iterate)
    cubic = contract("mik,mkj->mij", iterate_full, square)
    fourth = contract("mki,mkj->mij", iterate_full, cubic)
    quintic = contract("mik,mkj->mij", iterate_full, fourth)
    return COEF_A * iterate + COEF_B * cubic + COEF_C * quintic


def per_device(
    weights, gradient, first_moment, second_moment, left_stat, right_stat, left_basis, right_basis
):
    width = gradient.shape[1] * lax.axis_size("shard")
    owned = (
        lax.all_to_all(weights, "shard", split_axis=0, concat_axis=1, tiled=True),
        lax.all_to_all(gradient, "shard", split_axis=0, concat_axis=1, tiled=True),
        lax.all_to_all(first_moment, "shard", split_axis=0, concat_axis=1, tiled=True),
        lax.all_to_all(second_moment, "shard", split_axis=0, concat_axis=1, tiled=True),
        lax.all_to_all(left_stat, "shard", split_axis=0, concat_axis=1, tiled=True),
        lax.all_to_all(right_stat, "shard", split_axis=0, concat_axis=1, tiled=True),
        lax.all_to_all(left_basis, "shard", split_axis=0, concat_axis=1, tiled=True),
        lax.all_to_all(right_basis, "shard", split_axis=0, concat_axis=1, tiled=True),
    )
    weight_own, grad_own, first_own, second_own, lstat_own, rstat_own, lbasis_own, rbasis_own = (
        owned
    )
    lbasis_full, grad_full = (
        lax.all_gather(lbasis_own, "tensor", axis=2, tiled=True),
        lax.all_gather(grad_own, "tensor", axis=2, tiled=True),
    )
    left_part = contract("mki,mkj->mij", lbasis_full, grad_own)
    left_full = lax.all_gather(left_part, "tensor", axis=2, tiled=True)
    rotated = contract("mik,mkj->mij", left_full, rbasis_own)
    first_new = BETA_ONE * first_own + (1.0 - BETA_ONE) * rotated
    second_new = BETA_TWO * second_own + (1.0 - BETA_TWO) * rotated * rotated
    direction = first_new / (jnp.sqrt(second_new) + ADAM_EPS)
    back_left = contract("mik,mkj->mij", lbasis_full, direction)
    back_term = contract("mik,mjk->mij", back_left, rbasis_own)
    grad_term = contract("mik,mjk->mij", grad_own, grad_own)
    update, outer = (
        lax.psum_scatter(back_term, "tensor", scatter_dimension=2, tiled=True),
        lax.psum_scatter(grad_term, "tensor", scatter_dimension=2, tiled=True),
    )
    weight_new = weight_own - STEP_RATE * update
    lstat_new = BETA_STAT * lstat_own + (1.0 - BETA_STAT) / width * outer
    inner = contract("mki,mkj->mij", grad_full, grad_own)
    rstat_new = BETA_STAT * rstat_own + (1.0 - BETA_STAT) / width * inner
    lstat_full, rstat_full = (
        lax.all_gather(lstat_new, "tensor", axis=2, tiled=True),
        lax.all_gather(rstat_new, "tensor", axis=2, tiled=True),
    )
    power_left = contract("mik,mkj->mij", lstat_full, lbasis_own)
    power_right = contract("mik,mkj->mij", rstat_full, rbasis_own)
    left_norm, right_norm = lax.psum(
        (
            jnp.sum(power_left * power_left, axis=(1, 2)),
            jnp.sum(power_right * power_right, axis=(1, 2)),
        ),
        "tensor",
    )
    iterate_left = power_left / jnp.sqrt(left_norm + NORM_EPS)[:, None, None]
    iterate_right = power_right / jnp.sqrt(right_norm + NORM_EPS)[:, None, None]
    for step in range(NS_STEPS):
        full_left, full_right = (
            lax.all_gather(iterate_left, "tensor", axis=2, tiled=True),
            lax.all_gather(iterate_right, "tensor", axis=2, tiled=True),
        )
        iterate_left = newton_step(iterate_left, full_left)
        iterate_right = newton_step(iterate_right, full_right)
    results = (
        lax.all_to_all(weight_new, "shard", split_axis=1, concat_axis=0, tiled=True),
        lax.all_to_all(first_new, "shard", split_axis=1, concat_axis=0, tiled=True),
        lax.all_to_all(second_new, "shard", split_axis=1, concat_axis=0, tiled=True),
        lax.all_to_all(lstat_new, "shard", split_axis=1, concat_axis=0, tiled=True),
        lax.all_to_all(rstat_new, "shard", split_axis=1, concat_axis=0, tiled=True),
        lax.all_to_all(iterate_left, "shard", split_axis=1, concat_axis=0, tiled=True),
        lax.all_to_all(iterate_right, "shard", split_axis=1, concat_axis=0, tiled=True),
    )
    return (results[0], results[1], results[2], results[3], results[4], results[5], results[6])


def solution(mesh):
    in_specs = (
        P(None, "shard", "tensor"),
        P(None, "shard", "tensor"),
        P(None, "shard", "tensor"),
        P(None, "shard", "tensor"),
        P(None, "shard", "tensor"),
        P(None, "shard", "tensor"),
        P(None, "shard", "tensor"),
        P(None, "shard", "tensor"),
    )
    out_specs = (
        P(None, "shard", "tensor"),
        P(None, "shard", "tensor"),
        P(None, "shard", "tensor"),
        P(None, "shard", "tensor"),
        P(None, "shard", "tensor"),
        P(None, "shard", "tensor"),
        P(None, "shard", "tensor"),
    )
    return jax.shard_map(
        per_device, mesh=mesh, in_specs=in_specs, out_specs=out_specs, check_vma=False
    )
```

profile of v0, /device:TPU:0, one launch (start us, length us, event | category | flops | bytes accessed | tf_op | source)
XLA Modules:
  0.0 501.7 jit_solution(6544706797960970972)
XLA Ops:
  7.2 30.4 %all_to_all.234 = f32[128,8,256]{2,1,0:T(8,128)S(1)} all-to-all(f32[128,8,256]{2,1,0:T(8,128)} %param.9), channel_id=1, replica_groups=mesh['shard'=64,'tensor'=2] {'shard'}, dimensions={0} | all-to-all | bytes 2097152 | tf_op jit(solution)/shard_map/all_to_all | solution.py:39
  42.1 22.2 %all_to_all.235 = f32[128,8,256]{2,1,0:T(8,128)S(1)} all-to-all(f32[128,8,256]{2,1,0:T(8,128)S(1)} %copy-done.30), channel_id=1, replica_groups=mesh['shard'=64,'tensor'=2] {'shard'}, dimensions={0} | all-to-all | bytes 2097152 | tf_op jit(solution)/shard_map/all_to_all | solution.py:43
  64.4 6.1 %fusion = f32[2,512,256]{2,1,0:T(8,128)} fusion(f32[2,512,512]{2,1,0:T(8,128)} %all-gather.20.cloned.1.call-done, f32[64,2,8,256]{3,2,1,0:T(8,128)S(1)} %bitcast.183, f32[64,2,8,256]{3,2,1,0:T(8,128)S(1)} %bitcast.175), kind=kOutput, calls=%fused_computation.12 | convolution fusion | flops 1611137024 | bytes 5242880 | tf_op jit(solution)/shard_map/mki,mkj->mij/dot_general | solution.py:22
  70.6 21.1 %all_to_all.236 = f32[128,8,256]{2,1,0:T(8,128)S(1)} all-to-all(f32[128,8,256]{2,1,0:T(8,128)S(1)} %copy-done.31), channel_id=1, replica_groups=mesh['shard'=64,'tensor'=2] {'shard'}, dimensions={0} | all-to-all | bytes 2097152 | tf_op jit(solution)/shard_map/all_to_all | solution.py:42
  94.2 20.3 %all_to_all.237 = f32[128,8,256]{2,1,0:T(8,128)S(1)} all-to-all(f32[128,8,256]{2,1,0:T(8,128)} %param.15), channel_id=1, replica_groups=mesh['shard'=64,'tensor'=2] {'shard'}, dimensions={0} | all-to-all | bytes 2097152 | tf_op jit(solution)/shard_map/all_to_all | solution.py:45
  124.0 10.1 %all-to-all-done.2 = f32[128,8,256]{2,1,0:T(8,128)S(1)} async-done(((f32[128,8,256]{2,1,0:T(8,128)}), f32[128,8,256]{2,1,0:T(8,128)S(1)}, u32[]{:S(2)}, u32[]{:S(2)}) %all-to-all-start.2) | async-done | bytes 1048608 | tf_op jit(solution)/shard_map/all_to_all | solution.py:44
  146.4 6.4 %all-gather.24.cloned.1.call-done = f32[2,512,512]{2,1,0:T(8,128)} async-done(((f32[2,512,256]{2,1,0:T(8,128)}), f32[2,512,512]{2,1,0:T(8,128)}) %all-gather.24.cloned.1.call-update) | async-done | bytes 2097168 | tf_op jit(solution)/shard_map/all_gather | solution.py:88
  220.2 6.0 %fusion.29 = f32[2,512,256]{2,1,0:T(8,128)} fusion(f32[2,512,512]{2,1,0:T(8,128)} %all-gather.16.cloned.1.call-done, f32[64,2,8,256]{3,2,1,0:T(8,128)S(1)} %bitcast.176), kind=kOutput, calls=%fused_computation.56 | convolution fusion | flops 1610612736 | bytes 4194304 | tf_op jit(solution)/shard_map/mki,mkj->mij/dot_general | solution.py:22
  226.7 10.2 %all-gather.28.cloned.1.call-done = f32[2,512,512]{2,1,0:T(8,128)} async-done(((f32[2,512,256]{2,1,0:T(8,128)}), f32[2,512,512]{2,1,0:T(8,128)}) %all-gather.28.cloned.1.call-update) | async-done | bytes 2097168 | tf_op jit(solution)/shard_map/all_gather | solution.py:88
  250.8 10.8 %all-to-all-start.5 = ((f32[128,8,256]{2,1,0:T(8,128)}), f32[128,8,256]{2,1,0:T(8,128)}, u32[]{:S(2)}, u32[]{:S(2)}) async-start(f32[128,8,256]{2,1,0:T(8,128)} %param.11), calls=%async_computation.5 | async-start | bytes 2097152 | tf_op jit(solution)/shard_map/all_to_all | solution.py:41
  274.6 6.2 %all-to-all-done.5 = f32[128,8,256]{2,1,0:T(8,128)} async-done(((f32[128,8,256]{2,1,0:T(8,128)}), f32[128,8,256]{2,1,0:T(8,128)}, u32[]{:S(2)}, u32[]{:S(2)}) %all-to-all-start.5) | async-done | bytes 1048608 | tf_op jit(solution)/shard_map/all_to_all | solution.py:41
  280.8 5.5 %all-to-all-start.1 = ((f32[128,8,256]{2,1,0:T(8,128)}), f32[128,8,256]{2,1,0:T(8,128)}, u32[]{:S(2)}, u32[]{:S(2)}) async-start(f32[128,8,256]{2,1,0:T(8,128)} %param.10), calls=%async_computation.1 | async-start | bytes 2097152 | tf_op jit(solution)/shard_map/all_to_all | solution.py:40
  292.9 11.4 %all-to-all-done.1 = f32[128,8,256]{2,1,0:T(8,128)} async-done(((f32[128,8,256]{2,1,0:T(8,128)}), f32[128,8,256]{2,1,0:T(8,128)}, u32[]{:S(2)}, u32[]{:S(2)}) %all-to-all-start.1) | async-done | bytes 1048608 | tf_op jit(solution)/shard_map/all_to_all | solution.py:40
  315.2 5.9 %all-to-all-start = ((f32[128,8,256]{2,1,0:T(8,128)}), f32[128,8,256]{2,1,0:T(8,128)}, u32[]{:S(2)}, u32[]{:S(2)}) async-start(f32[128,8,256]{2,1,0:T(8,128)} %param.8), calls=%async_computation | async-start | bytes 2097152 | tf_op jit(solution)/shard_map/all_to_all | solution.py:38
  331.2 7.2 %all-to-all-done = f32[128,8,256]{2,1,0:T(8,128)} async-done(((f32[128,8,256]{2,1,0:T(8,128)}), f32[128,8,256]{2,1,0:T(8,128)}, u32[]{:S(2)}, u32[]{:S(2)}) %all-to-all-start) | async-done | bytes 1048608 | tf_op jit(solution)/shard_map/all_to_all | solution.py:38
  338.4 5.5 %all-to-all-start.12 = ((f32[2,512,256]{2,0,1:T(2,128)}), f32[2,512,256]{2,0,1:T(2,128)}, u32[]{:S(2)}, u32[]{:S(2)}) async-start(f32[2,512,256]{2,0,1:T(2,128)} %copy.48), calls=%async_computation.14 | async-start | bytes 2097152 | tf_op jit(solution)/shard_map/all_to_all | solution.py:98
  360.0 6.3 %all-to-all-start.10 = ((f32[2,512,256]{2,0,1:T(2,128)}), f32[2,512,256]{2,0,1:T(2,128)}, u32[]{:S(2)}, u32[]{:S(2)}) async-start(f32[2,512,256]{2,0,1:T(2,128)} %copy.44), calls=%async_computation.12 | async-start | bytes 2097152 | tf_op jit(solution)/shard_map/all_to_all | solution.py:97
  376.3 5.5 %all-to-all-done.10 = f32[2,512,256]{2,0,1:T(2,128)} async-done(((f32[2,512,256]{2,0,1:T(2,128)}), f32[2,512,256]{2,0,1:T(2,128)}, u32[]{:S(2)}, u32[]{:S(2)}) %all-to-all-start.10) | async-done | bytes 1048608 | tf_op jit(solution)/shard_map/all_to_all | solution.py:97
  381.8 5.5 %all-to-all-start.7 = ((f32[2,512,256]{2,0,1:T(2,128)}), f32[2,512,256]{2,0,1:T(2,128)}, u32[]{:S(2)}, u32[]{:S(2)}) async-start(f32[2,512,256]{2,0,1:T(2,128)} %copy.39), calls=%async_computation.8 | async-start | bytes 2097152 | tf_op jit(solution)/shard_map/all_to_all | solution.py:95
  402.2 7.1 %all-to-all-start.8 = ((f32[2,512,256]{2,0,1:T(2,128)}), f32[2,512,256]{2,0,1:T(2,128)}, u32[]{:S(2)}, u32[]{:S(2)}) async-start(f32[2,512,256]{2,0,1:T(2,128)} %copy.41), calls=%async_computation.9 | async-start | bytes 2097152 | tf_op jit(solution)/shard_map/all_to_all | solution.py:96
  423.9 8.4 %all-to-all-start.6 = ((f32[2,512,256]{2,0,1:T(2,128)}), f32[2,512,256]{2,0,1:T(2,128)}, u32[]{:S(2)}, u32[]{:S(2)}) async-start(f32[2,512,256]{2,0,1:T(2,128)} %copy.37), calls=%async_computation.7 | async-start | bytes 2097152 | tf_op jit(solution)/shard_map/all_to_all | solution.py:94
  441.1 6.0 %fusion.57 = f32[2,512,256]{2,1,0:T(8,128)} fusion(f32[2,512,512]{2,1,0:T(8,128)} %all-gather.44.cloned.1.call-done, f32[2,512,256]{2,1,0:T(8,128)S(1)} %copy-done.16), kind=kOutput, calls=%fused_computation.84 | convolution fusion | flops 1610612736 | bytes 4194304 | tf_op jit(solution)/shard_map/mki,mkj->mij/dot_general | solution.py:22
  447.1 11.0 %all-to-all-start.13 = ((f32[2,512,256]{2,0,1:T(2,128)}), f32[2,512,256]{2,0,1:T(2,128)}, u32[]{:S(2)}, u32[]{:S(2)}) async-start(f32[2,512,256]{2,0,1:T(2,128)} %copy.50), calls=%async_computation.15 | async-start | bytes 2097152 | tf_op jit(solution)/shard_map/all_to_all | solution.py:99
  472.7 6.6 %all-to-all-start.14 = ((f32[2,512,256]{2,0,1:T(2,128)}), f32[2,512,256]{2,0,1:T(2,128)S(1)}, u32[]{:S(2)}, u32[]{:S(2)}) async-start(f32[2,512,256]{2,0,1:T(2,128)} %copy.52), calls=%async_computation.16 | async-start | bytes 2097152 | tf_op jit(solution)/shard_map/all_to_all | solution.py:100
  (192 shorter events, 244.8 us)
Async XLA Ops:
  7.2 57.2 %all-gather.20.cloned.1.call-start = ((), (), s32[]{:S(2)}) async-start(), calls=%async_computation.21 | async-start | bytes 3145728 | tf_op jit(solution)/shard_map/all_gather | solution.py:52
  38.7 53.1 %reduce-scatter.5.cloned.1.call-start = ((), (), s32[]{:S(2)}) async-start(), calls=%async_computation.20 | async-start | bytes 3145728 | tf_op jit(solution)/shard_map/reduce_scatter | solution.py:65
  42.0 77.4 %all-gather.34.cloned.1.call-start = ((), (), s32[]{:S(2)}) async-start(), calls=%async_computation.28 | async-start | bytes 3145728 | tf_op jit(solution)/shard_map/all_gather | solution.py:73
  70.5 63.5 %all-gather.22.cloned.1.call-start = ((), (), s32[]{:S(2)}) async-start(), calls=%async_computation.22 | async-start | bytes 3145728 | tf_op jit(solution)/shard_map/all_gather | solution.py:72
  119.2 33.6 %all-gather.24.cloned.1.call-start = ((), (), s32[]{:S(2)}) async-start(), calls=%async_computation.23 | async-start | bytes 3145728 | tf_op jit(solution)/shard_map/all_gather | solution.py:88
  143.8 25.7 %all-gather.36.cloned.1.call-start = ((), (), s32[]{:S(2)}) async-start(), calls=%async_computation.29 | async-start | bytes 3145728 | tf_op jit(solution)/shard_map/all_gather | solution.py:89
  146.3 40.1 %all-gather.26.cloned.1.call-start = ((), (), s32[]{:S(2)}) async-start(), calls=%async_computation.24 | async-start | bytes 3145728 | tf_op jit(solution)/shard_map/all_gather | solution.py:88
  166.8 36.5 %all-gather.38.cloned.1.call-start = ((), (), s32[]{:S(2)}) async-start(), calls=%async_computation.30 | async-start | bytes 3145728 | tf_op jit(solution)/shard_map/all_gather | solution.py:89
  183.4 36.7 %all-gather.16.cloned.1.call-start = ((), (), s32[]{:S(2)}) async-start(), calls=%async_computation.17 | async-start | bytes 3145728 | tf_op jit(solution)/shard_map/all_gather | solution.py:51
  185.9 51.0 %all-gather.28.cloned.1.call-start = ((), (), s32[]{:S(2)}) async-start(), calls=%async_computation.25 | async-start | bytes 3145728 | tf_op jit(solution)/shard_map/all_gather | solution.py:88
  200.3 61.4 %all-gather.40.cloned.1.call-start = ((), (), s32[]{:S(2)}) async-start(), calls=%async_computation.31 | async-start | bytes 3145728 | tf_op jit(solution)/shard_map/all_gather | solution.py:89
  217.5 88.2 %all-gather.18.cloned.1.call-start = ((), (), s32[]{:S(2)}) async-start(), calls=%async_computation.18 | async-start | bytes 3145728 | tf_op jit(solution)/shard_map/all_gather | solution.py:55
  226.2 96.7 %all-gather.30.cloned.1.call-start = ((), (), s32[]{:S(2)}) async-start(), calls=%async_computation.26 | async-start | bytes 3145728 | tf_op jit(solution)/shard_map/all_gather | solution.py:88
  250.8 30.0 %all-to-all-start.5 = ((f32[128,8,256]{2,1,0:T(8,128)}), f32[128,8,256]{2,1,0:T(8,128)}, u32[]{:S(2)}, u32[]{:S(2)}) async-start(f32[128,8,256]{2,1,0:T(8,128)} %param.11), calls=%async_computation.5 | async-start | bytes 2097152 | tf_op jit(solution)/shard_map/all_to_all | solution.py:41
  280.8 23.5 %all-to-all-start.1 = ((f32[128,8,256]{2,1,0:T(8,128)}), f32[128,8,256]{2,1,0:T(8,128)}, u32[]{:S(2)}, u32[]{:S(2)}) async-start(f32[128,8,256]{2,1,0:T(8,128)} %param.10), calls=%async_computation.1 | async-start | bytes 2097152 | tf_op jit(solution)/shard_map/all_to_all | solution.py:40
  286.4 81.7 %all-gather.42.cloned.1.call-start = ((), (), s32[]{:S(2)}) async-start(), calls=%async_computation.32 | async-start | bytes 3145728 | tf_op jit(solution)/shard_map/all_gather | solution.py:89
  291.4 118.0 %reduce-scatter.3.cloned.1.call-start = ((), (), s32[]{:S(2)}) async-start(), calls=%async_computation.19 | async-start | bytes 3145728 | tf_op jit(solution)/shard_map/reduce_scatter | solution.py:64
  315.2 23.2 %all-to-all-start = ((f32[128,8,256]{2,1,0:T(8,128)}), f32[128,8,256]{2,1,0:T(8,128)}, u32[]{:S(2)}, u32[]{:S(2)}) async-start(f32[128,8,256]{2,1,0:T(8,128)} %param.8), calls=%async_computation | async-start | bytes 2097152 | tf_op jit(solution)/shard_map/all_to_all | solution.py:38
  343.9 69.0 %all-gather.32.cloned.1.call-start = ((), (), s32[]{:S(2)}) async-start(), calls=%async_computation.27 | async-start | bytes 3145728 | tf_op jit(solution)/shard_map/all_gather | solution.py:88
  360.0 21.8 %all-to-all-start.10 = ((f32[2,512,256]{2,0,1:T(2,128)}), f32[2,512,256]{2,0,1:T(2,128)}, u32[]{:S(2)}, u32[]{:S(2)}) async-start(f32[2,512,256]{2,0,1:T(2,128)} %copy.44), calls=%async_computation.12 | async-start | bytes 2097152 | tf_op jit(solution)/shard_map/all_to_all | solution.py:97
  387.4 53.7 %all-gather.44.cloned.1.call-start = ((), (), s32[]{:S(2)}) async-start(), calls=%async_computation.33 | async-start | bytes 3145728 | tf_op jit(solution)/shard_map/all_gather | solution.py:89
  402.2 21.7 %all-to-all-start.8 = ((f32[2,512,256]{2,0,1:T(2,128)}), f32[2,512,256]{2,0,1:T(2,128)}, u32[]{:S(2)}, u32[]{:S(2)}) async-start(f32[2,512,256]{2,0,1:T(2,128)} %copy.41), calls=%async_computation.9 | async-start | bytes 2097152 | tf_op jit(solution)/shard_map/all_to_all | solution.py:96
  423.9 23.3 %all-to-all-start.6 = ((f32[2,512,256]{2,0,1:T(2,128)}), f32[2,512,256]{2,0,1:T(2,128)}, u32[]{:S(2)}, u32[]{:S(2)}) async-start(f32[2,512,256]{2,0,1:T(2,128)} %copy.37), calls=%async_computation.7 | async-start | bytes 2097152 | tf_op jit(solution)/shard_map/all_to_all | solution.py:94
  447.1 25.5 %all-to-all-start.13 = ((f32[2,512,256]{2,0,1:T(2,128)}), f32[2,512,256]{2,0,1:T(2,128)}, u32[]{:S(2)}, u32[]{:S(2)}) async-start(f32[2,512,256]{2,0,1:T(2,128)} %copy.50), calls=%async_computation.15 | async-start | bytes 2097152 | tf_op jit(solution)/shard_map/all_to_all | solution.py:99
  (36 other events, 270.3 us)
Sparse Core Ops, SparseCore 0:
  38.8 8.9 all-gather.19
  50.1 13.7 reduce-scatter.4
  70.7 10.1 all-gather.33
  94.3 8.7 all-gather.21
  143.9 8.8 all-gather.23
  154.9 14.6 all-gather.35
  171.8 14.6 all-gather.25
  188.6 14.6 all-gather.37
  205.5 14.6 all-gather.15
  222.2 14.6 all-gather.27
  239.1 14.6 all-gather.39
  255.9 14.6 all-gather.17
  272.7 14.6 all-gather.29
  291.5 14.4 all-gather.41
  315.3 8.1 reduce-scatter.2
  352.5 14.4 all-gather.31
  395.7 14.4 all-gather.43
where the time goes:
time: 512 us; the launch traced here: 502 us
  matrix products  183 us (36%)
  blocking collectives  96.5 us (19%)
  waiting for transfers between devices  81.3 us (16%)
  starting transfers between devices  80.5 us (16%)
  local copies, waits for them, and re-layouts  34.2 us (7%)
  between operations  14.9 us (3%)
  other arithmetic  11.7 us (2%)
    dot_general x48, matrix products, contract(): jnp.einsum(form, left, right, precision=HIGH, preferred_element_type=jnp....  183 us
    all_to_all x1, blocking collectives, per_device(): lax.all_to_all(gradient, 'shard', split_axis=0, concat_axis=1, tiled=True)  30.4 us
    all_to_all x1, blocking collectives, per_device(): lax.all_to_all(right_stat, 'shard', split_axis=0, concat_axis=1, tiled=True)  22.2 us
    all_to_all x1, blocking collectives, per_device(): lax.all_to_all(left_stat, 'shard', split_axis=0, concat_axis=1, tiled=True)  21.1 us
    all_to_all x1, blocking collectives, per_device(): lax.all_to_all(right_basis, 'shard', split_axis=0, concat_axis=1, tiled=T...  20.3 us
    all_gather x5, waiting for transfers between devices, per_device(): lax.all_gather(iterate_left, 'tensor', axis=2, tiled=True)  16.8 us
    all_to_all x1, waiting for transfers between devices, per_device(): lax.all_to_all(first_moment, 'shard', split_axis=0, concat_axis=1, tiled=...  11.4 us
    all_to_all x1, starting transfers between devices, per_device(): lax.all_to_all(iterate_left, 'shard', split_axis=1, concat_axis=0, tiled=...  11 us
  transfers between devices with their start and end apart: 28, of which 16 were waited for; matrix products, arithmetic and copies ran while one was open for 43% of the time, Pallas kernels for 0%

commit v1 on v0

v1 whole, which is shorter than its diff:
```python
import functools

import jax
import jax.numpy as jnp
from jax import lax
from jax.experimental import pallas as pl
from jax.experimental.pallas import tpu as pltpu
from jax.sharding import PartitionSpec as P

NS_STEPS = 5

BETA_ONE = 0.9
BETA_TWO = 0.99
BETA_STAT = 0.95
ADAM_EPS = 1e-08
STEP_RATE = 0.01
NORM_EPS = 1e-06
COEF_A = 3.4445
COEF_B = -4.775
COEF_C = 2.0315

MESH = pl.DeviceIdType.MESH
NN = (((1,), (0,)), ((), ()))
NT = (((1,), (1,)), ((), ()))

GRAD, LBAS, RBAS, LSTAT, RSTAT, ROT, DIR, UPD, NLSTAT, NRSTAT, NLBAS, NRBAS = range(12)


def split(value):
    head = value.astype(jnp.bfloat16)
    return head, (value - head.astype(jnp.float32)).astype(jnp.bfloat16)


def product(left, right, form):
    (lh, ll), (rh, rl) = left, right
    dot = functools.partial(
        lax.dot_general, dimension_numbers=form, preferred_element_type=jnp.float32
    )
    return dot(lh, rh) + (dot(lh, rl) + dot(ll, rh))


def kernel(
    n_shard,
    n_tensor,
    grad,
    first,
    second,
    weights,
    lstat,
    rstat,
    lbasis,
    rbasis,
    out_weights,
    out_first,
    out_second,
    out_lstat,
    out_rstat,
    out_lbasis,
    out_rbasis,
    g_own,
    basis_own,
    stat_own,
    dir_own,
    rot_send,
    upd_send,
    rot_recv,
    dir_send,
    upd_recv,
    moments,
    iterate,
    work,
    g_head,
    g_tail,
    b_head,
    b_tail,
    x_head,
    x_tail,
    s_head,
    s_tail,
    send_sem,
    recv_sem,
    load_sem,
):
    order = n_shard * n_tensor
    mats, rows, cols = grad.shape
    width = g_own.shape[1]
    half = width // 2
    shard, tensor = lax.axis_index("shard"), lax.axis_index("tensor")
    me = shard * n_tensor + tensor

    def place(d):
        return d // n_tensor, lax.rem(d, n_tensor)

    def block(d):
        s, t = place(d)
        return (
            pl.ds(pl.multiple_of(s * rows, rows), rows),
            pl.ds(pl.multiple_of(t * cols, cols), cols),
        )

    def to_owners(source, target, index):
        mine = block(me)
        pltpu.make_async_copy(source.at[me], target.at[mine], recv_sem.at[index]).start()

        def send(k, carry):
            d = lax.rem(me + k, order)
            pltpu.make_async_remote_copy(
                src_ref=source.at[d],
                dst_ref=target.at[mine],
                send_sem=send_sem.at[index],
                recv_sem=recv_sem.at[index],
                device_id=place(d),
                device_id_type=MESH,
            ).start()
            return carry

        lax.fori_loop(1, order, send, 0)

    def to_rows(source, target, index):
        pltpu.make_async_copy(source.at[block(me)], target.at[me], recv_sem.at[index]).start()

        def send(k, carry):
            d = lax.rem(me + k, order)
            pltpu.make_async_remote_copy(
                src_ref=source.at[block(d)],
                dst_ref=target.at[me],
                send_sem=send_sem.at[index],
                recv_sem=recv_sem.at[index],
                device_id=place(d),
                device_id_type=MESH,
            ).start()
            return carry

        lax.fori_loop(1, order, send, 0)

    def arrived(target, index):
        pltpu.make_async_remote_copy(
            src_ref=target,
            dst_ref=target,
            send_sem=send_sem.at[index],
            recv_sem=recv_sem.at[index],
            device_id=place(lax.rem(me + 1, order)),
            device_id_type=MESH,
        ).wait_recv()

    def chunks(body):
        def step(i, carry):
            body(pl.ds(pl.multiple_of(i * half, half), half))
            return carry

        lax.fori_loop(0, 2, step, 0)

    barrier = pltpu.get_barrier_semaphore()

    def greet(k, carry):
        pl.semaphore_signal(
            barrier, inc=1, device_id=place(lax.rem(me + k, order)), device_id_type=MESH
        )
        return carry

    lax.fori_loop(1, order, greet, 0)
    pl.semaphore_wait(barrier, order - 1)

    to_owners(grad, g_own, GRAD)
    to_owners(lbasis, basis_own.at[0], LBAS)
    to_owners(rbasis, basis_own.at[1], RBAS)
    to_owners(lstat, stat_own.at[0], LSTAT)
    to_owners(rstat, stat_own.at[1], RSTAT)
    loads = [
        pltpu.make_async_copy(source, moments.at[i], load_sem.at[i])
        for i, source in enumerate((first, second, weights))
    ]
    for load in loads:
        load.start()

    arrived(g_own, GRAD)
    scale = (1.0 - BETA_STAT) / width
    g_head[0], g_tail[0] = split(g_own[...])
    g_head[1], g_tail[1] = split(g_own[...].T)

    def gram(side, carry):
        def rows_of(r):
            full = g_head[side], g_tail[side]
            part = g_head[side, r, :], g_tail[side, r, :]
            work[side, r, :] = scale * product(part, full, NT)

        chunks(rows_of)
        return carry

    lax.fori_loop(0, 2, gram, 0)

    arrived(basis_own.at[0], LBAS)
    b_head[0], b_tail[0] = split(basis_own[0])
    x_head[0], x_tail[0] = split(basis_own[0].T)

    def left_rotate(r):
        part = product((x_head[0, r, :], x_tail[0, r, :]), (g_head[0], g_tail[0]), NN)
        s_head[r, :], s_tail[r, :] = split(part)

    chunks(left_rotate)
    arrived(basis_own.at[1], RBAS)
    b_head[1], b_tail[1] = split(basis_own[1])

    def right_rotate(r):
        rot_send[r, :] = product(
            (s_head[r, :], s_tail[r, :]), (b_head[1], b_tail[1]), NN
        )

    chunks(right_rotate)
    to_rows(rot_send, rot_recv, ROT)

    def power(side, carry):
        arrived(stat_own.at[side], LSTAT + side)
        stat_own[side] = BETA_STAT * stat_own[side] + work[side]
        s_head[...], s_tail[...] = split(stat_own[side])

        def rows_of(r):
            iterate[side, r, :] = product(
                (s_head[r, :], s_tail[r, :]), (b_head[side], b_tail[side]), NN
            )

        chunks(rows_of)
        for which, target in enumerate((out_lstat, out_rstat)):

            @pl.when(side == which)
            def _():
                to_rows(stat_own.at[which], target, NLSTAT + which)

        value = iterate[side]
        value = value / jnp.sqrt(jnp.sum(value * value) + NORM_EPS)
        iterate[side] = value
        x_head[side], x_tail[side] = split(value)
        return carry

    lax.fori_loop(0, 2, power, 0)

    def newton(side):
        def step(_, carry):
            def squares(r):
                full = x_head[side], x_tail[side]
                value = product((x_head[side, r, :], x_tail[side, r, :]), full, NT)
                work[0, r, :] = value
                s_head[r, :], s_tail[r, :] = split(value)

            chunks(squares)

            def polynomial(r):
                fourth = product((s_head[r, :], s_tail[r, :]), (s_head[...], s_tail[...]), NN)
                value = COEF_B * work[0, r, :] + COEF_C * fourth
                g_head[0, r, :], g_tail[0, r, :] = split(value)

            chunks(polynomial)

            def combine(r):
                full = x_head[side], x_tail[side]
                value = product((g_head[0, r, :], g_tail[0, r, :]), full, NN)
                iterate[side, r, :] = COEF_A * iterate[side, r, :] + value

            chunks(combine)
            x_head[side], x_tail[side] = split(iterate[side])
            return carry

        lax.fori_loop(0, NS_STEPS, step, 0)

    def refresh(side, carry):
        newton(side)
        for which, target in enumerate((out_lbasis, out_rbasis)):

            @pl.when(side == which)
            def _():
                to_rows(iterate.at[which], target, NLBAS + which)

        @pl.when(side == 0)
        def _():
            arrived(rot_recv, ROT)
            for load in loads:
                load.wait()

            def adam(i, inner):
                m = pl.ds(i * 8, 8)
                rotated = rot_recv[m]
                new_first = BETA_ONE * moments[0, m] + (1.0 - BETA_ONE) * rotated
                new_second = BETA_TWO * moments[1, m] + (1.0 - BETA_TWO) * rotated * rotated
                out_first[m] = new_first
                out_second[m] = new_second
                dir_send[m] = new_first / (jnp.sqrt(new_second) + ADAM_EPS)
                return inner

            lax.fori_loop(0, mats // 8, adam, 0)
            to_owners(dir_send, dir_own, DIR)

        return carry

    lax.fori_loop(0, 2, refresh, 0)

    arrived(dir_own, DIR)
    g_head[1], g_tail[1] = split(dir_own[...])

    def left_back(r):
        part = product((b_head[0, r, :], b_tail[0, r, :]), (g_head[1], g_tail[1]), NN)
        s_head[r, :], s_tail[r, :] = split(part)

    chunks(left_back)

    def right_back(r):
        upd_send[r, :] = product(
            (s_head[r, :], s_tail[r, :]), (b_head[1], b_tail[1]), NT
        )

    chunks(right_back)
    to_rows(upd_send, upd_recv, UPD)
    arrived(upd_recv, UPD)

    def descend(i, carry):
        m = pl.ds(i * 8, 8)
        out_weights[m] = moments[2, m] - STEP_RATE * upd_recv[m]
        return carry

    lax.fori_loop(0, mats // 8, descend, 0)

    arrived(out_lstat, NLSTAT)
    arrived(out_rstat, NRSTAT)
    arrived(out_lbasis, NLBAS)
    arrived(out_rbasis, NRBAS)

    def sent(index, carry):
        part = rot_recv.at[pl.ds(0, order - 1)]
        pltpu.make_async_remote_copy(
            src_ref=part,
            dst_ref=part,
            send_sem=send_sem.at[index],
            recv_sem=recv_sem.at[index],
            device_id=place(lax.rem(me + 1, order)),
            device_id_type=MESH,
        ).wait_send()
        return carry

    lax.fori_loop(0, 12, sent, 0)


def per_device(
    weights, gradient, first_moment, second_moment, left_stat, right_stat, left_basis, right_basis
):
    n_shard, n_tensor = lax.axis_size("shard"), lax.axis_size("tensor")
    mats, rows, cols = gradient.shape
    width = rows * n_shard
    f32, bf16 = jnp.float32, jnp.bfloat16
    kept = jax.ShapeDtypeStruct((mats, rows, cols), f32)
    vmem = pl.BlockSpec(memory_space=pltpu.VMEM)

    def whole(*lead, dtype=f32):
        return pltpu.VMEM((*lead, width, width), dtype)

    def strip(*lead):
        return pltpu.VMEM((*lead, mats, rows, cols), f32)

    return pl.pallas_call(
        functools.partial(kernel, n_shard, n_tensor),
        out_shape=(kept,) * 7,
        in_specs=[pl.BlockSpec(memory_space=pl.ANY)] * 8,
        out_specs=[vmem] * 7,
        scratch_shapes=[
            whole(),
            whole(2),
            whole(2),
            whole(),
            whole(),
            whole(),
            strip(),
            strip(),
            strip(),
            strip(3),
            whole(2),
            whole(2),
            *[whole(2, dtype=bf16) for _ in range(6)],
            *[whole(dtype=bf16) for _ in range(2)],
            pltpu.SemaphoreType.DMA((12,)),
            pltpu.SemaphoreType.DMA((12,)),
            pltpu.SemaphoreType.DMA((3,)),
        ],
        compiler_params=pltpu.CompilerParams(
            collective_id=0, has_side_effects=True, vmem_limit_bytes=40 * 1024 * 1024
        ),
        name="soap_step",
    )(
        gradient,
        first_moment,
        second_moment,
        weights,
        left_stat,
        right_stat,
        left_basis,
        right_basis,
    )


def solution(mesh):
    spec = P(None, "shard", "tensor")
    return jax.shard_map(
        per_device, mesh=mesh, in_specs=(spec,) * 8, out_specs=(spec,) * 7, check_vma=False
    )
```

time: 512 us -> 177 us (0.35); the launches traced: 502 us -> 174 us
  matrix products: 183 us -> 0 us
  Pallas kernels: 0 us -> 159 us
  blocking collectives: 96.5 us -> 0 us
  waiting for transfers between devices: 81.3 us -> 0 us
  starting transfers between devices: 80.5 us -> 0 us
  local copies, waits for them, and re-layouts: 34.2 us -> 14.1 us
  between operations: 14.9 us -> 0.66 us
  other arithmetic: 11.7 us -> 0 us
    dot_general x48 -> x0, matrix products: 183 us -> none  [contract(): jnp.einsum(form, left, right, precision=HIGH, preferred_element_type=jnp....]
    pallas_call x0 -> x1, Pallas kernels: none -> 159 us  [per_device(): pl.pallas_call(functools.partial(kernel, n_shard, n_tensor), out_shape=(k...]
    all_to_all x4 -> x0, blocking collectives: 94 us -> none  [the longest x1 30.4 us: per_device(): lax.all_to_all(gradient, 'shard', split_axis=0, concat_axis=1, tiled=True)]
    all_to_all x11 -> x0, starting transfers between devices: 77.4 us -> none  [the longest x1 11 us: per_device(): lax.all_to_all(iterate_left, 'shard', split_axis=1, concat_axis=0, tiled=...]
    all_to_all x11 -> x0, waiting for transfers between devices: 56.4 us -> none  [the longest x1 11.4 us: per_device(): lax.all_to_all(first_moment, 'shard', split_axis=0, concat_axis=1, tiled=...]
    all_gather x15 -> x0, waiting for transfers between devices: 24.6 us -> none  [the longest x5 16.8 us: per_device(): lax.all_gather(iterate_left, 'tensor', axis=2, tiled=True)]
    all_to_all x9 -> x0, local copies, waits for them, and re-layouts: 18.1 us -> none  [the longest x1 2.42 us: per_device(): lax.all_to_all(left_basis, 'shard', split_axis=0, concat_axis=1, tiled=True)]
    add x6 -> x0, local copies, waits for them, and re-layouts: 13.2 us -> none  [the longest x2 3.56 us: newton_step(): return COEF_A * iterate + COEF_B * cubic + COEF_C * quintic]
  transfers between devices with their start and end apart: 28 -> 0, of which waited for: 16 -> 0; matrix products, arithmetic and copies ran while one was open for 43% -> 0% of each run, Pallas kernels for 0% -> 0%
where the time goes in v1:
time: 177 us; the launch traced here: 174 us
  Pallas kernels  159 us (90%)
  local copies, waits for them, and re-layouts  14.1 us (8%)
    pallas_call x1, Pallas kernels, per_device(): pl.pallas_call(functools.partial(kernel, n_shard, n_tensor), out_shape=(k...  159 us
    unnamed x19, local copies, waits for them, and re-layouts  14.1 us

profile of v1, /device:TPU:0, one launch (start us, length us, event | category | flops | bytes accessed | tf_op | source)
XLA Modules:
  0.0 173.8 jit_solution(1711996016284674587)
XLA Ops:
  0.6 0.0 copy-start
  0.6 1.2 copy-done
  1.9 0.0 copy-start.1
  1.9 1.2 copy-done.1
  3.1 0.0 copy-start.2
  3.1 1.2 copy-done.2
  4.3 0.0 copy-start.3
  4.3 1.2 copy-done.3
  5.5 0.0 copy-start.4
  5.5 1.2 copy-done.4
  6.8 0.0 copy-start.5
  6.8 1.2 copy-done.5
  8.0 159.0 %soap_step.1 = (f32[128,8,256]{2,1,0:T(8,128)S(1)}, f32[128,8,256]{2,1,0:T(8,128)S(1)}, f32[128,8,256]{2,1,0:T(8,128)S(1)}, f32[128,8,256]{2,1,0:T(8,128)S(1)}, ...) custom-call(f32[128,8,256]{2,1,0:T(8,128)S(1)} %copy-done, ...), custom_call_target="tpu_custom_call" | custom-call | tf_op jit(solution)/shard_map/soap_step/pallas_call | solution.py:357
  167.0 1.0 copy.22
  168.0 1.0 copy.23
  169.0 1.0 copy.24
  169.9 1.0 copy.25
  170.9 1.0 copy.26
  171.9 1.0 copy.27
  172.9 1.0 copy.28
Async XLA Ops:
  0.6 1.2 copy-start
  1.9 1.2 copy-start.1
  3.1 1.2 copy-start.2
  4.3 1.2 copy-start.3
  5.5 1.2 copy-start.4
  6.8 1.2 copy-start.5

commit v2 on v1

--- a/solution.py
+++ b/solution.py
@@ -19,6 +19,8 @@
 COEF_B = -4.775
 COEF_C = 2.0315
 
+STRIDE = 37
+LANES = 128
 MESH = pl.DeviceIdType.MESH
 NN = (((1,), (0,)), ((), ()))
 NT = (((1,), (1,)), ((), ()))
@@ -88,50 +90,95 @@
     shard, tensor = lax.axis_index("shard"), lax.axis_index("tensor")
     me = shard * n_tensor + tensor
 
-    def place(d):
-        return d // n_tensor, lax.rem(d, n_tensor)
-
-    def block(d):
-        s, t = place(d)
+    def to_peers(send):
+        def around(j, carry):
+            s = lax.rem(shard + j * STRIDE, n_shard)
+            for t in range(n_tensor):
+                send(s * n_tensor + t, s, t)
+            return carry
+
+        for t in range(1, n_tensor):
+            other = lax.rem(tensor + t, n_tensor)
+            send(shard * n_tensor + other, shard, other)
+        lax.fori_loop(1, n_shard, around, 0)
+
+    def block(s, t):
         return (
             pl.ds(pl.multiple_of(s * rows, rows), rows),
             pl.ds(pl.multiple_of(t * cols, cols), cols),
         )
 
-    def to_owners(source, target, index):
-        mine = block(me)
-        pltpu.make_async_copy(source.at[me], target.at[mine], recv_sem.at[index]).start()
-
-        def send(k, carry):
-            d = lax.rem(me + k, order)
+    def exchange(source_of, target, own, index):
+        pltpu.make_async_copy(own, target, recv_sem.at[index]).start()
+
+        def send(d, s, t):
             pltpu.make_async_remote_copy(
-                src_ref=source.at[d],
-                dst_ref=target.at[mine],
+                src_ref=source_of(d, s, t),
+                dst_ref=target,
                 send_sem=send_sem.at[index],
                 recv_sem=recv_sem.at[index],
-                device_id=place(d),
+                device_id=(s, t),
                 device_id_type=MESH,
             ).start()
-            return carry
-
-        lax.fori_loop(1, order, send, 0)
+
+        to_peers(send)
+
+    def to_owners(source, target, index):
+        exchange(
+            lambda d, s, t: source.at[d], target.at[block(shard, tensor)], source.at[me], index
+        )
 
     def to_rows(source, target, index):
-        pltpu.make_async_copy(source.at[block(me)], target.at[me], recv_sem.at[index]).start()
-
-        def send(k, carry):
-            d = lax.rem(me + k, order)
-            pltpu.make_async_remote_copy(
-                src_ref=source.at[block(d)],
-                dst_ref=target.at[me],
-                send_sem=send_sem.at[index],
-                recv_sem=recv_sem.at[index],
-                device_id=place(d),
-                device_id_type=MESH,
-            ).start()
-            return carry
-
-        lax.fori_loop(1, order, send, 0)
+        exchange(
+            lambda d, s, t: source.at[block(s, t)],
+            target.at[me],
+            source.at[block(shard, tensor)],
+            index,
+        )
+
+    blocks = width // LANES
+    row_block = shard * rows // LANES
+    wide = cols // LANES
+    count = blocks * (blocks + 1) // 2
+
+    def travels(row, lag, side):
+        if blocks % 2:
+            return lag <= blocks // 2
+        late = row >= blocks // 2 if side else row < blocks // 2
+        return (lag < blocks // 2) | ((lag == blocks // 2) & late)
+
+    def stat_parts(side, body):
+        flags = []
+        for i in range(wide):
+            lag = lax.rem(tensor * wide + i - row_block + blocks, blocks)
+            flags.append(travels(row_block, lag, side))
+        for i, flag in enumerate(flags):
+            pl.when(flag)(functools.partial(body, i * LANES, LANES))
+
+    def stat_to_owners(source, side):
+        target = stat_own.at[side]
+        down, across = block(shard, tensor)
+
+        def body(start, lanes):
+            part = pl.ds(start, lanes)
+            to = target.at[down, pl.ds(pl.multiple_of(tensor * cols + start, lanes), lanes)]
+            exchange(
+                lambda d, s, t: source.at[d, :, part],
+                to,
+                source.at[me, :, part],
+                LSTAT + side,
+            )
+
+        stat_parts(side, body)
+
+    def mirror(side):
+        for row in range(blocks):
+            for lag in range(blocks):
+                if not travels(row, lag, side):
+                    column = (row + lag) % blocks
+                    down = slice(row * LANES, (row + 1) * LANES)
+                    across = slice(column * LANES, (column + 1) * LANES)
+                    stat_own[side, down, across] = stat_own[side, across, down].T
 
     def arrived(target, index):
         pltpu.make_async_remote_copy(
@@ -139,7 +186,7 @@
             dst_ref=target,
             send_sem=send_sem.at[index],
             recv_sem=recv_sem.at[index],
-            device_id=place(lax.rem(me + 1, order)),
+            device_id=(lax.rem(shard + 1, n_shard), tensor),
             device_id_type=MESH,
         ).wait_recv()
 
@@ -152,20 +199,18 @@
 
     barrier = pltpu.get_barrier_semaphore()
 
-    def greet(k, carry):
-        pl.semaphore_signal(
-            barrier, inc=1, device_id=place(lax.rem(me + k, order)), device_id_type=MESH
-        )
-        return carry
-
-    lax.fori_loop(1, order, greet, 0)
+    to_peers(
+        lambda d, s, t: pl.semaphore_signal(
+            barrier, inc=1, device_id=(s, t), device_id_type=MESH
+        )
+    )
     pl.semaphore_wait(barrier, order - 1)
 
     to_owners(grad, g_own, GRAD)
     to_owners(lbasis, basis_own.at[0], LBAS)
     to_owners(rbasis, basis_own.at[1], RBAS)
-    to_owners(lstat, stat_own.at[0], LSTAT)
-    to_owners(rstat, stat_own.at[1], RSTAT)
+    stat_to_owners(lstat, 0)
+    stat_to_owners(rstat, 1)
     loads = [
         pltpu.make_async_copy(source, moments.at[i], load_sem.at[i])
         for i, source in enumerate((first, second, weights))
@@ -210,7 +255,9 @@
     to_rows(rot_send, rot_recv, ROT)
 
     def power(side, carry):
-        arrived(stat_own.at[side], LSTAT + side)
+        arrived(stat_own.at[side, pl.ds(0, count * LANES * LANES // width)], LSTAT + side)
+        for which in range(2):
+            pl.when(side == which)(functools.partial(mirror, which))
         stat_own[side] = BETA_STAT * stat_own[side] + work[side]
         s_head[...], s_tail[...] = split(stat_own[side])
 
@@ -323,19 +370,39 @@
     arrived(out_lbasis, NLBAS)
     arrived(out_rbasis, NRBAS)
 
-    def sent(index, carry):
-        part = rot_recv.at[pl.ds(0, order - 1)]
+    def sent(part, index):
         pltpu.make_async_remote_copy(
             src_ref=part,
             dst_ref=part,
             send_sem=send_sem.at[index],
             recv_sem=recv_sem.at[index],
-            device_id=place(lax.rem(me + 1, order)),
+            device_id=(lax.rem(shard + 1, n_shard), tensor),
             device_id_type=MESH,
         ).wait_send()
-        return carry
-
-    lax.fori_loop(0, 12, sent, 0)
+
+    for index in range(12):
+        if index not in (LSTAT, RSTAT):
+            sent(rot_recv.at[pl.ds(0, order - 1)], index)
+    for side in range(2):
+        stat_parts(
+            side,
+            lambda start, lanes: sent(
+                rot_recv.at[pl.ds(0, order - 1), :, pl.ds(0, lanes)], LSTAT + side
+            ),
+        )
+
+
+def keep(*refs):
+    count = len(refs) // 2
+    sem = refs[-1]
+    copies = [
+        pltpu.make_async_copy(source, target, sem.at[i])
+        for i, (source, target) in enumerate(zip(refs[:count], refs[count:]))
+    ]
+    for copy in copies:
+        copy.start()
+    for copy in copies:
+        copy.wait()
 
 
 def per_device(
@@ -347,6 +414,7 @@
     f32, bf16 = jnp.float32, jnp.bfloat16
     kept = jax.ShapeDtypeStruct((mats, rows, cols), f32)
     vmem = pl.BlockSpec(memory_space=pltpu.VMEM)
+    hbm = pl.BlockSpec(memory_space=pltpu.HBM)
 
     def whole(*lead, dtype=f32):
         return pltpu.VMEM((*lead, width, width), dtype)
@@ -354,10 +422,10 @@
     def strip(*lead):
         return pltpu.VMEM((*lead, mats, rows, cols), f32)
 
-    return pl.pallas_call(
+    results = pl.pallas_call(
         functools.partial(kernel, n_shard, n_tensor),
         out_shape=(kept,) * 7,
-        in_specs=[pl.BlockSpec(memory_space=pl.ANY)] * 8,
+        in_specs=[hbm] * 8,
         out_specs=[vmem] * 7,
         scratch_shapes=[
             whole(),
@@ -379,7 +447,7 @@
             pltpu.SemaphoreType.DMA((3,)),
         ],
         compiler_params=pltpu.CompilerParams(
-            collective_id=0, has_side_effects=True, vmem_limit_bytes=40 * 1024 * 1024
+            collective_id=0, has_side_effects=True, vmem_limit_bytes=46 * 1024 * 1024
         ),
         name="soap_step",
     )(
@@ -392,6 +460,15 @@
         left_basis,
         right_basis,
     )
+    return pl.pallas_call(
+        keep,
+        out_shape=(kept,) * 7,
+        in_specs=[vmem] * 7,
+        out_specs=[hbm] * 7,
+        scratch_shapes=[pltpu.SemaphoreType.DMA((7,))],
+        compiler_params=pltpu.CompilerParams(vmem_limit_bytes=1024 * 1024),
+        name="keep",
+    )(*results)
 
 
 def solution(mesh):

time: 177 us -> 147 us (0.83); the launches traced: 174 us -> 146 us
  local copies, waits for them, and re-layouts: 14.1 us -> 0 us
  Pallas kernels: 159 us -> 146 us
    pallas_call x1, Pallas kernels: 159 us -> 142 us  [per_device(): pl.pallas_call(functools.partial(kernel, n_shard, n_tensor), out_shape=(k...]
    unnamed x19 -> x0, local copies, waits for them, and re-layouts: 14.1 us -> none
    pallas_call x0 -> x1, Pallas kernels: none -> 3.05 us  [per_device(): pl.pallas_call(keep, out_shape=(kept,) * 7, in_specs=[vmem] * 7, out_spec...]
where the time goes in v2:
time: 147 us; the launch traced here: 146 us
  Pallas kernels  146 us (99%)
    pallas_call x1, Pallas kernels, per_device(): pl.pallas_call(functools.partial(kernel, n_shard, n_tensor), out_shape=(k...  142 us
    pallas_call x1, Pallas kernels, per_device(): pl.pallas_call(keep, out_shape=(kept,) * 7, in_specs=[vmem] * 7, out_spec...  3.05 us

profile of v2, /device:TPU:0, one launch (start us, length us, event | category | flops | bytes accessed | tf_op | source)
XLA Modules:
  0.0 146.2 jit_solution(5510582654415179114)
XLA Ops:
  0.6 142.5 %soap_step.1 = (f32[128,8,256]{2,1,0:T(8,128)S(1)}, f32[128,8,256]{2,1,0:T(8,128)S(1)}, f32[128,8,256]{2,1,0:T(8,128)S(1)}, f32[128,8,256]{2,1,0:T(8,128)S(1)}, ...) custom-call(f32[128,8,256]{2,1,0:T(8,128)} %grad.1, f32[128,8,256]{2,1,0:T(8,128)} %first.1, ...), custom_call_target="tpu_custom_call" | custom-call | tf_op jit(solution)/shard_map/soap_step/pallas_call | solution.py:425
  143.1 3.0 %keep.1 = (f32[128,8,256]{2,1,0:T(8,128)}, f32[128,8,256]{2,1,0:T(8,128)}, f32[128,8,256]{2,1,0:T(8,128)}, f32[128,8,256]{2,1,0:T(8,128)}, f32[128,8,256]{2,1,0:...) custom-call(f32[128,8,256]{2,1,0:T(8,128)S(1)} %get-tuple-element.14.refs_0_, ...), custom_call_target="tpu_custom_call" | custom-call | tf_op jit(solution)/shard_map/keep/pallas_call | solution.py:463

commit v3 on v2

--- a/solution.py
+++ b/solution.py
@@ -1,4 +1,5 @@
 import functools
+import itertools
 
 import jax
 import jax.numpy as jnp
@@ -21,6 +22,7 @@
 
 STRIDE = 37
 LANES = 128
+PARTS = 4
 MESH = pl.DeviceIdType.MESH
 NN = (((1,), (0,)), ((), ()))
 NT = (((1,), (1,)), ((), ()))
@@ -90,9 +92,11 @@
     shard, tensor = lax.axis_index("shard"), lax.axis_index("tensor")
     me = shard * n_tensor + tensor
 
+    stride = STRIDE + tensor * (n_shard - 2 * STRIDE)
+
     def to_peers(send):
         def around(j, carry):
-            s = lax.rem(shard + j * STRIDE, n_shard)
+            s = lax.rem(shard + j * stride, n_shard)
             for t in range(n_tensor):
                 send(s * n_tensor + t, s, t)
             return carry
@@ -199,11 +203,21 @@
 
     barrier = pltpu.get_barrier_semaphore()
 
-    to_peers(
-        lambda d, s, t: pl.semaphore_signal(
-            barrier, inc=1, device_id=(s, t), device_id_type=MESH
-        )
+    edge = round(n_shard ** (1 / 3))
+    here = shard // (edge * edge), lax.rem(shard // edge, edge), lax.rem(shard, edge)
+    along = [[lax.rem(at + step, edge) for step in range(edge)] for at in here]
+    steps = sorted(
+        itertools.product(range(edge), repeat=3),
+        key=lambda step: -sum(min(i, edge - i) for i in step),
     )
+    for i, j, k in steps:
+        s = (along[0][i] * edge + along[1][j]) * edge + along[2][k]
+        for t in range(n_tensor):
+            if (i, j, k) == (0, 0, 0):
+                if t == 0:
+                    continue
+                t = lax.rem(tensor + t, n_tensor)
+            pl.semaphore_signal(barrier, inc=1, device_id=(s, t), device_id_type=MESH)
     pl.semaphore_wait(barrier, order - 1)
 
     to_owners(grad, g_own, GRAD)
@@ -395,8 +409,12 @@
 def keep(*refs):
     count = len(refs) // 2
     sem = refs[-1]
+    part = refs[0].shape[0] // PARTS
     copies = [
-        pltpu.make_async_copy(source, target, sem.at[i])
+        pltpu.make_async_copy(
+            source.at[pl.ds(p * part, part)], target.at[pl.ds(p * part, part)], sem.at[i, p]
+        )
+        for p in range(PARTS)
         for i, (source, target) in enumerate(zip(refs[:count], refs[count:]))
     ]
     for copy in copies:
@@ -465,7 +483,7 @@
         out_shape=(kept,) * 7,
         in_specs=[vmem] * 7,
         out_specs=[hbm] * 7,
-        scratch_shapes=[pltpu.SemaphoreType.DMA((7,))],
+        scratch_shapes=[pltpu.SemaphoreType.DMA((7, PARTS))],
         compiler_params=pltpu.CompilerParams(vmem_limit_bytes=1024 * 1024),
         name="keep",
     )(*results)

time: 147 us -> 146 us (level)
  no operation moved by 1% of the time
where the time goes in v3:
time: 146 us; the launch traced here: 145 us
  Pallas kernels  145 us (99%)
    pallas_call x1, Pallas kernels, per_device(): pl.pallas_call(functools.partial(kernel, n_shard, n_tensor), out_shape=(k...  142 us
    pallas_call x1, Pallas kernels, per_device(): pl.pallas_call(keep, out_shape=(kept,) * 7, in_specs=[vmem] * 7, out_spec...  3.19 us

profile of v3, /device:TPU:0, one launch (start us, length us, event | category | flops | bytes accessed | tf_op | source)
XLA Modules:
  0.0 145.3 jit_solution(6117888985943892448)
XLA Ops:
  0.6 141.5 %soap_step.1 = (f32[128,8,256]{2,1,0:T(8,128)S(1)}, f32[128,8,256]{2,1,0:T(8,128)S(1)}, f32[128,8,256]{2,1,0:T(8,128)S(1)}, f32[128,8,256]{2,1,0:T(8,128)S(1)}, ...) custom-call(f32[128,8,256]{2,1,0:T(8,128)} %grad.1, f32[128,8,256]{2,1,0:T(8,128)} %first.1, ...), custom_call_target="tpu_custom_call" | custom-call | tf_op jit(solution)/shard_map/soap_step/pallas_call | solution.py:443
  142.1 3.2 %keep.1 = (f32[128,8,256]{2,1,0:T(8,128)}, f32[128,8,256]{2,1,0:T(8,128)}, f32[128,8,256]{2,1,0:T(8,128)}, f32[128,8,256]{2,1,0:T(8,128)}, f32[128,8,256]{2,1,0:...) custom-call(f32[128,8,256]{2,1,0:T(8,128)S(1)} %get-tuple-element.14.refs_0_, ...), custom_call_target="tpu_custom_call" | custom-call | tf_op jit(solution)/shard_map/keep/pallas_call | solution.py:481
